TPU v7x, 32 devices: a whole 2x2x4 slice. The times are simulated.
32 devices in a mesh: gx: 8 (over z, core), gy: 4 (over y, x).
Axes of the slice: x: 2, y: 2, z: 4, core: 2. Of those that a mesh axis runs over, the one named last changes fastest.
Arguments:
- mesh_state: bfloat16 [128, 128, 32, 128], P('gx', 'gy'), may hold values from -6 to 6
- part_feat: bfloat16 [131072, 128], P(('gx', 'gy')), may hold values from -6 to 6
- cell_index: int32 [131072], P(('gx', 'gy')), may hold values from 0 to 16383, as said below
- pairs: int32 [2, 786432], P(None, ('gx', 'gy')), may hold values from 0 to 4095, as said below
- dest: int32 [131072], P(('gx', 'gy')), may hold values from 0 to 8, as said below
- mass: float32 [131072], P(('gx', 'gy')), may hold values from 0.5 to 2
- velocity: float32 [3, 131072], P(None, ('gx', 'gy')), may hold values from -30 to 30
- w_enc: bfloat16 [128, 128], replicated, may hold values from -0.5 to 0.5
- w_mesh: bfloat16 [128, 128], replicated, may hold values from -0.21875 to 0.21875
- w_pair: bfloat16 [128, 256], replicated, may hold values from -0.5 to 0.5
- w_edge: bfloat16 [128, 128], replicated, may hold values from -0.5 to 0.5
- w_node: bfloat16 [256, 128], replicated, may hold values from -0.25 to 0.25
- w_accel: bfloat16 [3, 128], replicated, may hold values from -0.5 to 0.5
Outputs:
- mesh_out: bfloat16 [128, 128, 32, 128], P('gx', 'gy')
- stay_feat: bfloat16 [131072, 128], P(('gx', 'gy'))
- stay_vel: float32 [3, 131072], P(None, ('gx', 'gy'))
- arrived_feat: bfloat16 [32768, 128], P(('gx', 'gy'))
- arrived_vel: float32 [4, 32768], P(None, ('gx', 'gy'))
Inputs may be any that keep to these rules, and one draw needn't show every extreme that they name: `dest`: 0 means the particle stays; k from 1 to 8 moves it in the k-th direction of the steps. At most 128 particles of one device take any one direction, and some device receives 128 particles from each of its eight neighbours. `cell_index`: A device's particles come in 8 aligned groups of 512 rows; the particles of group g lie in cells g * 2048 to (g + 1) * 2048 - 1 of the device's block. `pairs`: A device's columns come in 8 aligned groups of 3072; both rows of a column of group g name particles of the device's group g, rows g * 512 to (g + 1) * 512 - 1.
All inputs are finite; a program needn't handle non-finite values.
Results may differ from a plain program's by a relative error of at most 0.0085.
Values may be sent and summed in bfloat16 or wider, within the bound.
A program may use at most 128 MiB of HBM per device.

v0:
```python
import jax
import jax.numpy as jnp
from jax import lax
from jax.sharding import PartitionSpec as P

directions = ((-1, -1), (-1, 0), (-1, 1), (0, -1), (0, 1), (1, -1), (1, 0), (1, 1))


def padded_2(array, sides, width):
    for axis, dim in sides:
        devices, length = (lax.axis_size(axis), array.shape[dim])
        up = [(i, (i + 1) % devices) for i in range(devices)]
        down = [(j, i) for i, j in up]
        last = lax.slice_in_dim(array, length - width, length, axis=dim)
        initial = lax.slice_in_dim(array, 0, width, axis=dim)
        before = lax.ppermute(last, axis, up)
        after = lax.ppermute(initial, axis, down)
        array = jnp.concatenate([before, array, after], axis=dim)
    return array


def from_behind(block, axis, distance):
    devices = range(lax.axis_size(axis))
    route = [((i - distance) % len(devices), i) for i in devices]
    return lax.ppermute(block, axis, route)


def group_sizes(parts, cells):
    members = min(512, parts)
    count = parts // members
    return (members, count, cells // count)


def encode(state_rows, feat, cell, w_enc):
    members, count, span = group_sizes(feat.shape[0], state_rows.shape[0])
    width = feat.shape[1]
    feat_g = feat.reshape(count, members, width)
    cell_g = cell.reshape(count, members)
    lanes = jnp.arange(span, dtype=jnp.int32)

    def encode_one_group(item):
        rows, cells, number = item
        onehot = ((cells - number * span)[:, None] == lanes[None, :]).astype(jnp.bfloat16)
        return lax.dot_general(
            onehot, rows, (((0,), (0,)), ((), ())), preferred_element_type=jnp.float32
        )

    numbers = jnp.arange(count, dtype=jnp.int32)
    deposit = (
        lax.map(encode_one_group, (feat_g, cell_g, numbers)).reshape(-1, width).astype(jnp.bfloat16)
    )
    return (
        state_rows.astype(jnp.float32) + jnp.dot(deposit, w_enc, preferred_element_type=jnp.float32)
    ).astype(jnp.bfloat16)


def zsides(field):
    padded = jnp.pad(field, [(0, 0)] * (field.ndim - 2) + [(1, 1), (0, 0)])
    return padded[..., 2:, :] + padded[..., :-2, :]


def mesh_update(centre, sides, w_mesh):
    width = centre.shape[-1]
    summed = sides.astype(jnp.bfloat16).reshape(-1, width)
    update = jnp.dot(summed, w_mesh, preferred_element_type=jnp.float32).reshape(centre.shape)
    return (centre.astype(jnp.float32) + jax.nn.silu(update)).astype(jnp.bfloat16)


def particle_step(feat, cell, pair, mesh_rows, w_pair, w_edge, w_node):
    width = feat.shape[1]
    channels = mesh_rows.shape[1]
    members, count, span = group_sizes(feat.shape[0], mesh_rows.shape[0])
    proj = jnp.dot(feat, w_pair, preferred_element_type=jnp.float32).astype(jnp.bfloat16)
    per_group = pair.shape[1] // count
    proj_g = proj.reshape(count, members, 2 * width)
    feat_g = feat.reshape(count, members, width)
    pair_g = pair.reshape(2, count, per_group).transpose(1, 0, 2)
    cell_g = cell.reshape(count, members)
    rows_g = mesh_rows.reshape(count, span, channels)
    lanes = jnp.arange(members, dtype=jnp.int32)
    cell_lanes = jnp.arange(span, dtype=jnp.int32)

    def particle_one_group(carry, item):
        proj_part, feat_part, pair_part, cell_part, mesh_part, number = item
        base = number * members
        send_hot = ((pair_part[0] - base)[:, None] == lanes[None, :]).astype(jnp.bfloat16)
        recv_hot = ((pair_part[1] - base)[:, None] == lanes[None, :]).astype(jnp.bfloat16)
        sent = jnp.dot(send_hot, proj_part[:, :width], preferred_element_type=jnp.float32)
        received = jnp.dot(recv_hot, proj_part[:, width:], preferred_element_type=jnp.float32)
        act = jax.nn.silu(sent + received).astype(jnp.bfloat16)
        message = jnp.dot(act, w_edge, preferred_element_type=jnp.float32)
        edge_sum = lax.dot_general(
            recv_hot.astype(jnp.float32),
            message,
            (((0,), (0,)), ((), ())),
            precision=lax.Precision.HIGHEST,
            preferred_element_type=jnp.float32,
        )
        edge_sum = edge_sum.astype(jnp.bfloat16)
        cell_hot = ((cell_part - number * span)[:, None] == cell_lanes[None, :]).astype(
            jnp.bfloat16
        )
        near = jnp.dot(cell_hot, mesh_part, preferred_element_type=jnp.float32).astype(jnp.bfloat16)
        update = jnp.dot(edge_sum, w_node[:width], preferred_element_type=jnp.float32)
        update = update + jnp.dot(near, w_node[width:], preferred_element_type=jnp.float32)
        return (carry, (feat_part.astype(jnp.float32) + jax.nn.silu(update)).astype(jnp.bfloat16))

    numbers = jnp.arange(count, dtype=jnp.int32)
    _, h_groups = lax.scan(particle_one_group, 0, (proj_g, feat_g, pair_g, cell_g, rows_g, numbers))
    return h_groups.reshape(-1, width)


def pack(h_new, vel1, mass, dest, cap):
    ways = jnp.arange(1, 9, dtype=jnp.int32)
    onehot = (dest[:, None] == ways[None, :]).astype(jnp.int32)
    slot = jnp.sum((jnp.cumsum(onehot, axis=0) - 1) * onehot, axis=1)
    extra = jnp.concatenate([vel1, mass[None, :]], axis=0).astype(jnp.bfloat16)
    slots = jnp.arange(cap, dtype=jnp.int32)
    feats = []
    moving = []
    for way in range(1, 9):
        chosen = ((dest == way)[None, :] & (slot[None, :] == slots[:, None])).astype(jnp.bfloat16)
        feats.append(
            jnp.dot(chosen, h_new, preferred_element_type=jnp.float32).astype(jnp.bfloat16)
        )
        moving.append(
            lax.dot_general(
                extra, chosen, (((1,), (1,)), ((), ())), preferred_element_type=jnp.float32
            ).astype(jnp.bfloat16)
        )
    return (jnp.stack(feats, axis=0), jnp.stack(moving, axis=0))


def unpack(moving, drift):
    values = moving.astype(jnp.float32)
    weight = values[..., 3:4, :]
    speed = jnp.where(weight > 0, values[..., :3, :] - drift[:, None], 0.0)
    return jnp.concatenate([speed, weight], axis=-2)


def shards(
    mesh_state,
    part_feat,
    cell_index,
    pairs,
    dest,
    mass,
    velocity,
    w_enc,
    w_mesh,
    w_pair,
    w_edge,
    w_node,
    w_accel,
):
    shape = mesh_state.shape
    width = part_feat.shape[1]
    mesh1 = encode(mesh_state.reshape(-1, shape[3]), part_feat, cell_index, w_enc).reshape(shape)
    padded = padded_2(mesh1, (("gx", 0), ("gy", 1)), 1)
    wide = padded.astype(jnp.float32)
    centre = wide[1:-1, 1:-1]
    sides = wide[:-2, 1:-1] + wide[2:, 1:-1] + wide[1:-1, :-2] + wide[1:-1, 2:] + zsides(centre)
    mesh2 = mesh_update(mesh1, sides, w_mesh)
    h_new = particle_step(
        part_feat, cell_index, pairs, mesh2.reshape(-1, shape[3]), w_pair, w_edge, w_node
    )
    accel = lax.dot_general(
        w_accel, h_new, (((1,), (1,)), ((), ())), preferred_element_type=jnp.float32
    )
    vel1 = velocity + accel
    momentum, total_mass = lax.psum(
        (jnp.sum(mass[None, :] * vel1, axis=1), jnp.sum(mass)), ("gx", "gy")
    )
    drift = momentum / total_mass
    staying = dest == 0
    stay_feat = jnp.where(staying[:, None], h_new, jnp.zeros_like(h_new))
    stay_vel = jnp.where(staying[None, :], vel1 - drift[:, None], 0.0)
    cap = part_feat.shape[0] // 32
    feats, moving = pack(h_new, vel1, mass, dest, cap)
    got_f = [feats[k] for k in range(8)]
    got_m = [moving[k] for k in range(8)]
    for step_x in (1, -1):
        chosen = [k for k, offset in enumerate(directions) if offset[0] == step_x]
        moved_f, moved_m = from_behind(
            (
                jnp.stack([got_f[k] for k in chosen], axis=0),
                jnp.stack([got_m[k] for k in chosen], axis=0),
            ),
            "gx",
            step_x,
        )
        for place, k in enumerate(chosen):
            got_f[k] = moved_f[place]
            got_m[k] = moved_m[place]
    for step_y in (1, -1):
        chosen = [k for k, offset in enumerate(directions) if offset[1] == step_y]
        moved_f, moved_m = from_behind(
            (
                jnp.stack([got_f[k] for k in chosen], axis=0),
                jnp.stack([got_m[k] for k in chosen], axis=0),
            ),
            "gy",
            step_y,
        )
        for place, k in enumerate(chosen):
            got_f[k] = moved_f[place]
            got_m[k] = moved_m[place]
    arrived_f = jnp.stack(got_f, axis=0)
    arrived_m = jnp.stack(got_m, axis=0)
    arrived_feat = arrived_f.reshape(-1, width)
    arrived_vel = unpack(arrived_m, drift).transpose(1, 0, 2).reshape(4, -1)
    return (mesh2, stay_feat, stay_vel, arrived_feat, arrived_vel)


def solution(mesh):
    placed = (
        P("gx", "gy", None, None),
        P(("gx", "gy"), None),
        P(("gx", "gy")),
        P(None, ("gx", "gy")),
        P(("gx", "gy")),
        P(("gx", "gy")),
        P(None, ("gx", "gy")),
        P(),
        P(),
        P(),
        P(),
        P(),
        P(),
    )
    return jax.shard_map(
        shards,
        mesh=mesh,
        in_specs=placed,
        out_specs=(
            P("gx", "gy", None, None),
            P(("gx", "gy"), None),
            P(None, ("gx", "gy")),
            P(("gx", "gy"), None),
            P(None, ("gx", "gy")),
        ),
        check_vma=False,
    )
```

profile of v0, /device:TPU:0, one launch (start us, length us, event | category | flops | bytes accessed | tf_op | source)
XLA Modules:
  0.0 347.9 jit_solution(7069706612158112352)
XLA Ops:
  1.4 34.5 %while.23 = (s32[]{:T(128)}, bf16[8,2048,128]{2,1,0:T(8,128)(2,1)}, s32[8,512]{1,0:T(8,128)S(1)}, s32[8]{0:T(128)S(1)}, bf16[8,512,128]{2,1,0:T(8,128)(2,1)}, /*index=5*/s32[]{:T(128)}, s32[1]{0:T(128)}) while((s32[]{:T(128)}, bf16[8,2048,128]{2,1,0:T(8,128)(2,1)}, s32[8,512]{1,0:T(8,128)S(1)}, s32[8]{0:T(128)S(1)}, ...), condition=%wide.region_1.2_spmd.clone, body=%wide.region_0.1_spmd.clone.sunk | while | flops 269484544 | bytes 1186925 | solution.py:50
  2.7 3.1 fusion.278
  7.0 3.1 fusion.278
  11.3 3.1 fusion.278
  15.6 3.1 fusion.278
  19.9 3.1 fusion.278
  24.2 3.1 fusion.278
  28.6 3.1 fusion.278
  32.9 3.1 fusion.278
  35.9 4.8 %fusion.48 = bf16[16384,128]{1,0:T(8,128)(2,1)S(1)} fusion(bf16[16384,128]{1,0:T(8,128)(2,1)} %bitcast.173, bf16[128,128]{1,0:T(8,128)(2,1)S(1)} %copy-done.11, bf16[16384,128]{1,0:T(8,128)(2,1)} %bitcast.172), kind=kOutput, calls=%fused_computation.48 | convolution fusion | flops 543162368 | bytes 12615680 | tf_op jit(solution)/shard_map/dot_general | solution.py:53
  40.8 2.0 copy-done.1
  43.3 4.1 %collective-permute-start.1 = (bf16[1,32,32,128]{3,2,1,0:T(8,128)(2,1)S(1)}, bf16[1,32,32,128]{3,2,1,0:T(8,128)(2,1)S(1)}, u32[]{:S(2)}, u32[]{:S(2)}) collective-permute-start(bf16[1,32,32,128]{3,2,1,0:T(8,128)(2,1)S(1)} %bitcast.189), channel_id=1, source_target_pairs={{4,0},{8,4},{12,8},{16,12},{20,16},{24,20},{28,24},{0,28},{5,1},{9... | collective-permute-start | bytes 786440 | tf_op jit(solution)/shard_map/ppermute | solution.py:17
  48.9 2.3 reduce-window.6
  52.1 1.8 pad_maximum_fusion.2
  53.9 2.1 collective-permute-start.2
  59.0 1.9 collective-permute-done.2
  60.9 3.9 %collective-permute-done.3 = bf16[18,1,32,128]{3,2,1,0:T(8,128)(2,1)} collective-permute-done((bf16[18,1,32,128]{3,2,1,0:T(8,128)(2,1)}, bf16[18,1,32,128]{3,2,1,0:T(8,128)(2,1)}, u32[]{:S(2)}, u32[]{:S(2)}) %collective-permute-start.3) | collective-permute-done | bytes 147488 | tf_op jit(solution)/shard_map/ppermute | solution.py:17
  64.8 4.2 %maximum_convert_fusion = f32[18,34,32,128]{3,2,1,0:T(8,128)S(1)} fusion(bf16[18,1,32,128]{3,2,1,0:T(8,128)(2,1)} %collective-permute-done.3, bf16[1,32,32,128]{3,2,1,0:T(8,128)(2,1)} %copy-done.5, bf16[16,32,32,128]{3,2,1,0:T(8,128)(2,1)} %bitcast.170, bf16[1,32,32,128]{3,2,1,0:T(8,128)(2,1)} %copy-done.4, bf16[18,1,32,128]{3,2,1,0:T(8,128)(2,1)} %collective-permute-done.2), kind=kLoop, calls=%fused_computation.59 | loop fusion | flops 12533760 | bytes 15040512 | tf_op jit(solution)/shard_map/convert_element_type | solution.py:160
  69.1 3.8 %copy-done.3 = f32[18,34,32,128]{3,2,1,0:T(8,128)} copy-done((f32[18,34,32,128]{3,2,1,0:T(8,128)}, f32[18,34,32,128]{3,2,1,0:T(8,128)S(1)}, u32[]{:S(2)}) %copy-start.3) | copy-done | bytes 10027032
  72.9 4.4 %slice.204 = f32[16,32,32,128]{3,2,1,0:T(8,128)} slice(f32[18,34,32,128]{3,2,1,0:T(8,128)S(1)} %maximum_convert_fusion), slice={[1:17], [1:33], [0:32], [0:128]} | slice | bytes 16777216 | tf_op jit(solution)/shard_map/slice | solution.py:161
  77.3 19.7 %add_convert_fusion = bf16[16,32,32,128]{3,2,1,0:T(8,128)(2,1)} fusion(bf16[16,32,32,128]{3,2,1,0:T(8,128)(2,1)S(1)} %bitcast.171, f32[16,32,32,128]{3,2,1,0:T(8,128)} %slice.204, f32[18,34,32,128]{3,2,1,0:T(8,128)} %copy-done.3, bf16[128,128]{1,0:T(8,128)(2,1)S(1)} %copy-done.21), kind=kOutput, calls=%fused_computation.57 | convolution fusion | flops 564133888 | bytes 50364416 | tf_op jit(solution)/shard_map/dot_general | solution.py:65
  97.5 166.0 %while.24 = (s32[]{:T(128)}, bf16[8,512,128]{2,1,0:T(8,128)(2,1)S(1)}, bf16[8,512,128]{2,1,0:T(8,128)(2,1)}, s32[8,2,3072]{2,1,0:T(2,128)}, s32[8]{0:T(128)}, /*...) while((s32[]{:T(128)}, ...), condition=%wide.region_3.4_spmd.clone.clone, body=%wide.region_2.3_spmd.clone.clone.sunk | while | flops 3632667136 | bytes 8842453 | solution.py:109
  100.9 2.6 fusion.287
  103.4 4.2 %fusion.288 = f32[3072,128]{1,0:T(8,128)} fusion(bf16[128,128]{1,0:T(8,128)(2,1)} %get-tuple-element.381, f32[3072,128]{1,0:T(8,128)} %fusion.287, s32[3072]{0:T(1024)} %bitcast.188, bf16[512,256]{1,0:T(8,128)(2,1)S(1)} %dynamic-slice_bitcast_fusion.2), kind=kOutput, calls=%fused_computation.25.clone.1 | convolution fusion | flops 507248640 | bytes 3321856 | tf_op jit(solution)/shard_map/while/body/eval_jaxpr/dot_general | solution.py:91
  107.7 6.9 %fusion.289 = bf16[512,128]{1,0:T(8,128)(2,1)S(1)} fusion(f32[3072,128]{1,0:T(8,128)} %fusion.288, s32[3072]{0:T(1024)S(1)} %bitcast.187), kind=kOutput, calls=%fused_computation.28.clone.1 | convolution fusion | flops 2417557504 | bytes 1716224 | tf_op jit(solution)/shard_map/while/body/eval_jaxpr/dot_general | solution.py:92
  116.1 2.1 fusion.291
  121.6 2.6 fusion.287
  124.2 4.2 %fusion.288 = f32[3072,128]{1,0:T(8,128)} fusion(bf16[128,128]{1,0:T(8,128)(2,1)} %get-tuple-element.381, f32[3072,128]{1,0:T(8,128)} %fusion.287, s32[3072]{0:T(1024)} %bitcast.188, bf16[512,256]{1,0:T(8,128)(2,1)S(1)} %dynamic-slice_bitcast_fusion.2), kind=kOutput, calls=%fused_computation.25.clone.1 | convolution fusion | flops 507248640 | bytes 3321856 | tf_op jit(solution)/shard_map/while/body/eval_jaxpr/dot_general | solution.py:91
  128.4 6.9 %fusion.289 = bf16[512,128]{1,0:T(8,128)(2,1)S(1)} fusion(f32[3072,128]{1,0:T(8,128)} %fusion.288, s32[3072]{0:T(1024)S(1)} %bitcast.187), kind=kOutput, calls=%fused_computation.28.clone.1 | convolution fusion | flops 2417557504 | bytes 1716224 | tf_op jit(solution)/shard_map/while/body/eval_jaxpr/dot_general | solution.py:92
  136.9 2.1 fusion.291
  142.4 2.6 fusion.287
  144.9 4.2 %fusion.288 = f32[3072,128]{1,0:T(8,128)} fusion(bf16[128,128]{1,0:T(8,128)(2,1)} %get-tuple-element.381, f32[3072,128]{1,0:T(8,128)} %fusion.287, s32[3072]{0:T(1024)} %bitcast.188, bf16[512,256]{1,0:T(8,128)(2,1)S(1)} %dynamic-slice_bitcast_fusion.2), kind=kOutput, calls=%fused_computation.25.clone.1 | convolution fusion | flops 507248640 | bytes 3321856 | tf_op jit(solution)/shard_map/while/body/eval_jaxpr/dot_general | solution.py:91
  149.2 6.9 %fusion.289 = bf16[512,128]{1,0:T(8,128)(2,1)S(1)} fusion(f32[3072,128]{1,0:T(8,128)} %fusion.288, s32[3072]{0:T(1024)S(1)} %bitcast.187), kind=kOutput, calls=%fused_computation.28.clone.1 | convolution fusion | flops 2417557504 | bytes 1716224 | tf_op jit(solution)/shard_map/while/body/eval_jaxpr/dot_general | solution.py:92
  157.6 2.1 fusion.291
  163.1 2.6 fusion.287
  165.7 4.2 %fusion.288 = f32[3072,128]{1,0:T(8,128)} fusion(bf16[128,128]{1,0:T(8,128)(2,1)} %get-tuple-element.381, f32[3072,128]{1,0:T(8,128)} %fusion.287, s32[3072]{0:T(1024)} %bitcast.188, bf16[512,256]{1,0:T(8,128)(2,1)S(1)} %dynamic-slice_bitcast_fusion.2), kind=kOutput, calls=%fused_computation.25.clone.1 | convolution fusion | flops 507248640 | bytes 3321856 | tf_op jit(solution)/shard_map/while/body/eval_jaxpr/dot_general | solution.py:91
  169.9 6.9 %fusion.289 = bf16[512,128]{1,0:T(8,128)(2,1)S(1)} fusion(f32[3072,128]{1,0:T(8,128)} %fusion.288, s32[3072]{0:T(1024)S(1)} %bitcast.187), kind=kOutput, calls=%fused_computation.28.clone.1 | convolution fusion | flops 2417557504 | bytes 1716224 | tf_op jit(solution)/shard_map/while/body/eval_jaxpr/dot_general | solution.py:92
  178.4 2.1 fusion.291
  183.9 2.6 fusion.287
  186.4 4.2 %fusion.288 = f32[3072,128]{1,0:T(8,128)} fusion(bf16[128,128]{1,0:T(8,128)(2,1)} %get-tuple-element.381, f32[3072,128]{1,0:T(8,128)} %fusion.287, s32[3072]{0:T(1024)} %bitcast.188, bf16[512,256]{1,0:T(8,128)(2,1)S(1)} %dynamic-slice_bitcast_fusion.2), kind=kOutput, calls=%fused_computation.25.clone.1 | convolution fusion | flops 507248640 | bytes 3321856 | tf_op jit(solution)/shard_map/while/body/eval_jaxpr/dot_general | solution.py:91
  190.6 6.9 %fusion.289 = bf16[512,128]{1,0:T(8,128)(2,1)S(1)} fusion(f32[3072,128]{1,0:T(8,128)} %fusion.288, s32[3072]{0:T(1024)S(1)} %bitcast.187), kind=kOutput, calls=%fused_computation.28.clone.1 | convolution fusion | flops 2417557504 | bytes 1716224 | tf_op jit(solution)/shard_map/while/body/eval_jaxpr/dot_general | solution.py:92
  199.1 2.1 fusion.291
  204.6 2.6 fusion.287
  207.2 4.2 %fusion.288 = f32[3072,128]{1,0:T(8,128)} fusion(bf16[128,128]{1,0:T(8,128)(2,1)} %get-tuple-element.381, f32[3072,128]{1,0:T(8,128)} %fusion.287, s32[3072]{0:T(1024)} %bitcast.188, bf16[512,256]{1,0:T(8,128)(2,1)S(1)} %dynamic-slice_bitcast_fusion.2), kind=kOutput, calls=%fused_computation.25.clone.1 | convolution fusion | flops 507248640 | bytes 3321856 | tf_op jit(solution)/shard_map/while/body/eval_jaxpr/dot_general | solution.py:91
  211.4 6.9 %fusion.289 = bf16[512,128]{1,0:T(8,128)(2,1)S(1)} fusion(f32[3072,128]{1,0:T(8,128)} %fusion.288, s32[3072]{0:T(1024)S(1)} %bitcast.187), kind=kOutput, calls=%fused_computation.28.clone.1 | convolution fusion | flops 2417557504 | bytes 1716224 | tf_op jit(solution)/shard_map/while/body/eval_jaxpr/dot_general | solution.py:92
  219.9 2.1 fusion.291
  225.4 2.6 fusion.287
  227.9 4.2 %fusion.288 = f32[3072,128]{1,0:T(8,128)} fusion(bf16[128,128]{1,0:T(8,128)(2,1)} %get-tuple-element.381, f32[3072,128]{1,0:T(8,128)} %fusion.287, s32[3072]{0:T(1024)} %bitcast.188, bf16[512,256]{1,0:T(8,128)(2,1)S(1)} %dynamic-slice_bitcast_fusion.2), kind=kOutput, calls=%fused_computation.25.clone.1 | convolution fusion | flops 507248640 | bytes 3321856 | tf_op jit(solution)/shard_map/while/body/eval_jaxpr/dot_general | solution.py:91
  232.1 6.9 %fusion.289 = bf16[512,128]{1,0:T(8,128)(2,1)S(1)} fusion(f32[3072,128]{1,0:T(8,128)} %fusion.288, s32[3072]{0:T(1024)S(1)} %bitcast.187), kind=kOutput, calls=%fused_computation.28.clone.1 | convolution fusion | flops 2417557504 | bytes 1716224 | tf_op jit(solution)/shard_map/while/body/eval_jaxpr/dot_general | solution.py:92
  240.6 2.1 fusion.291
  246.1 2.6 fusion.287
  248.7 4.2 %fusion.288 = f32[3072,128]{1,0:T(8,128)} fusion(bf16[128,128]{1,0:T(8,128)(2,1)} %get-tuple-element.381, f32[3072,128]{1,0:T(8,128)} %fusion.287, s32[3072]{0:T(1024)} %bitcast.188, bf16[512,256]{1,0:T(8,128)(2,1)S(1)} %dynamic-slice_bitcast_fusion.2), kind=kOutput, calls=%fused_computation.25.clone.1 | convolution fusion | flops 507248640 | bytes 3321856 | tf_op jit(solution)/shard_map/while/body/eval_jaxpr/dot_general | solution.py:91
  252.9 6.9 %fusion.289 = bf16[512,128]{1,0:T(8,128)(2,1)S(1)} fusion(f32[3072,128]{1,0:T(8,128)} %fusion.288, s32[3072]{0:T(1024)S(1)} %bitcast.187), kind=kOutput, calls=%fused_computation.28.clone.1 | convolution fusion | flops 2417557504 | bytes 1716224 | tf_op jit(solution)/shard_map/while/body/eval_jaxpr/dot_general | solution.py:92
  261.4 2.1 fusion.291
  264.9 40.4 %all-reduce.1 = (f32[3]{0:T(128)S(1)}, f32[]{:T(128)}) all-reduce(f32[3]{0:T(128)S(1)} %get-tuple-element.226, f32[]{:T(128)} %get-tuple-element.212), channel_id=1, replica_groups=mesh['gx'=8,'gy'=4] {'gx','gy'}, use_global_device_ids=true, to_apply=%region_5.6 | all-reduce | flops 4 | bytes 32 | tf_op jit(solution)/shard_map/psum | solution.py:171
  317.6 2.9 broadcast_select_fusion
  320.6 3.5 %collective-permute-start.8 = (bf16[3,4,128]{2,1,0:T(4,128)(2,1)S(1)}, bf16[3,4,128]{2,1,0:T(4,128)(2,1)S(1)}, u32[]{:S(2)}, u32[]{:S(2)}) collective-permute-start(bf16[3,4,128]{2,1,0:T(4,128)(2,1)S(1)} %pad_maximum_fusion.8), channel_id=1, source_target_pairs={{4,0},{8,4},{12,8},{16,12},{20,16},{24,20},{28,24},{0,28},{5,1},{9... | collective-permute-start | bytes 9224 | tf_op jit(solution)/shard_map/ppermute | solution.py:25
  325.4 3.5 collective-permute-start.10
  330.2 2.1 collective-permute-start.11
  332.3 2.2 collective-permute-start.4
  335.2 1.6 collective-permute-done.4
  338.4 3.1 collective-permute-done.6
  341.5 1.6 collective-permute-start.7
  343.7 3.4 collective-permute-done.7
  (180 shorter events, 60.5 us)
Async XLA Ops:
  0.6 46.8 %copy-start = (bf16[128,256]{1,0:T(8,128)(2,1)S(1)}, bf16[128,256]{1,0:T(8,128)(2,1)}, u32[]{:S(2)}) copy-start(bf16[128,256]{1,0:T(8,128)(2,1)} %param.26) | copy-start | bytes 196612
  1.4 34.5 %copy-start.11 = (bf16[128,128]{1,0:T(8,128)(2,1)S(1)}, bf16[128,128]{1,0:T(8,128)(2,1)}, u32[]{:S(2)}) copy-start(bf16[128,128]{1,0:T(8,128)(2,1)} %param.24) | copy-start | bytes 98308
  35.9 4.8 %copy-start.9 = (s32[8,512]{1,0:T(8,128)}, s32[8,512]{1,0:T(8,128)S(1)}, u32[]{:S(2)}) copy-start(s32[8,512]{1,0:T(8,128)S(1)} %get-tuple-element.403) | copy-start | bytes 49156
  35.9 11.5 %copy-start.6 = (bf16[8,512,128]{2,1,0:T(8,128)(2,1)S(1)}, bf16[8,512,128]{2,1,0:T(8,128)(2,1)}, u32[]{:S(2)}) copy-start(bf16[8,512,128]{2,1,0:T(8,128)(2,1)} %get-tuple-element.392) | copy-start | bytes 3145732
  40.7 2.0 copy-start.1
  42.8 5.4 %copy-start.8 = (s32[4096]{0:T(1024)S(1)}, s32[4096]{0:T(1024)}, u32[]{:S(2)}) copy-start(s32[4096]{0:T(1024)} %param.21) | copy-start | bytes 49156
  42.8 9.0 %collective-permute-start = (bf16[1,32,32,128]{3,2,1,0:T(8,128)(2,1)S(1)}, bf16[1,32,32,128]{3,2,1,0:T(8,128)(2,1)S(1)}, u32[]{:S(2)}, u32[]{:S(2)}) collective-permute-start(bf16[1,32,32,128]{3,2,1,0:T(8,128)(2,1)S(1)} %bitcast.190), channel_id=1, source_target_pairs={{0,4},{4,8},{8,12},{12,16},{16,20},{20,24},{24,28},{28,0},{1,5},{5... | collective-permute-start | bytes 786440 | tf_op jit(solution)/shard_map/ppermute | solution.py:16
  43.3 8.7 %collective-permute-start.1 = (bf16[1,32,32,128]{3,2,1,0:T(8,128)(2,1)S(1)}, bf16[1,32,32,128]{3,2,1,0:T(8,128)(2,1)S(1)}, u32[]{:S(2)}, u32[]{:S(2)}) collective-permute-start(bf16[1,32,32,128]{3,2,1,0:T(8,128)(2,1)S(1)} %bitcast.189), channel_id=1, source_target_pairs={{4,0},{8,4},{12,8},{16,12},{20,16},{24,20},{28,24},{0,28},{5,1},{9... | collective-permute-start | bytes 786440 | tf_op jit(solution)/shard_map/ppermute | solution.py:17
  47.4 9.6 %copy-start.10 = (f32[4096]{0:T(1024)S(1)}, f32[4096]{0:T(1024)}, u32[]{:S(2)}) copy-start(f32[4096]{0:T(1024)} %param.22) | copy-start | bytes 49156
  51.8 5.2 %copy-start.4 = (bf16[1,32,32,128]{3,2,1,0:T(8,128)(2,1)}, bf16[1,32,32,128]{3,2,1,0:T(8,128)(2,1)S(1)}, u32[]{:S(2)}) copy-start(bf16[1,32,32,128]{3,2,1,0:T(8,128)(2,1)S(1)} %collective-permute-done) | copy-start | bytes 786436
  52.1 4.9 %copy-start.5 = (bf16[1,32,32,128]{3,2,1,0:T(8,128)(2,1)}, bf16[1,32,32,128]{3,2,1,0:T(8,128)(2,1)S(1)}, u32[]{:S(2)}) copy-start(bf16[1,32,32,128]{3,2,1,0:T(8,128)(2,1)S(1)} %collective-permute-done.1) | copy-start | bytes 786436
  53.9 7.0 %collective-permute-start.2 = (bf16[18,1,32,128]{3,2,1,0:T(8,128)(2,1)}, bf16[18,1,32,128]{3,2,1,0:T(8,128)(2,1)}, u32[]{:S(2)}, u32[]{:S(2)}) collective-permute-start(bf16[18,1,32,128]{3,2,1,0:T(8,128)(2,1)} %get-tuple-element.201), channel_id=1, source_target_pairs={{0,1},{1,2},{2,3},{3,0},{4,5},{5,6},{6,7},{7,4},{8,9},{9,10},{10,1... | collective-permute-start | bytes 442376 | tf_op jit(solution)/shard_map/ppermute | solution.py:16
  56.0 8.8 %collective-permute-start.3 = (bf16[18,1,32,128]{3,2,1,0:T(8,128)(2,1)}, bf16[18,1,32,128]{3,2,1,0:T(8,128)(2,1)}, u32[]{:S(2)}, u32[]{:S(2)}) collective-permute-start(bf16[18,1,32,128]{3,2,1,0:T(8,128)(2,1)} %get-tuple-element.202), channel_id=1, source_target_pairs={{1,0},{2,1},{3,2},{0,3},{5,4},{6,5},{7,6},{4,7},{9,8},{10,9},{11,1... | collective-permute-start | bytes 442376 | tf_op jit(solution)/shard_map/ppermute | solution.py:17
  69.1 3.9 %copy-start.3 = (f32[18,34,32,128]{3,2,1,0:T(8,128)}, f32[18,34,32,128]{3,2,1,0:T(8,128)S(1)}, u32[]{:S(2)}) copy-start(f32[18,34,32,128]{3,2,1,0:T(8,128)S(1)} %maximum_convert_fusion) | copy-start | bytes 30081028
  72.9 4.4 %copy-start.2 = (bf16[16384,128]{1,0:T(8,128)(2,1)S(1)}, bf16[16384,128]{1,0:T(8,128)(2,1)}, u32[]{:S(2)}) copy-start(bf16[16384,128]{1,0:T(8,128)(2,1)} %copy-done.1) | copy-start | bytes 12582916
  72.9 4.4 %copy-start.21 = (bf16[128,128]{1,0:T(8,128)(2,1)S(1)}, bf16[128,128]{1,0:T(8,128)(2,1)}, u32[]{:S(2)}) copy-start(bf16[128,128]{1,0:T(8,128)(2,1)} %param.25) | copy-start | bytes 98308
  77.3 20.2 %copy-start.7 = (bf16[256,128]{1,0:T(8,128)(2,1)S(1)}, bf16[256,128]{1,0:T(8,128)(2,1)}, u32[]{:S(2)}) copy-start(bf16[256,128]{1,0:T(8,128)(2,1)} %param.28) | copy-start | bytes 196612
  263.5 46.5 %copy-start.12 = (s32[4096]{0:T(1024)S(1)}, s32[4096]{0:T(1024)}, u32[]{:S(2)}) copy-start(s32[4096]{0:T(1024)} %fusion.226) | copy-start | bytes 49156
  263.5 46.5 %copy-start.20 = (pred[4096]{0:T(1024)(128)(4,1)S(1)}, pred[4096]{0:T(1024)(128)(4,1)}, u32[]{:S(2)}) copy-start(pred[4096]{0:T(1024)(128)(4,1)} %get-tuple-element.214) | copy-start | bytes 12292
  263.5 47.6 %copy-start.19 = (pred[4096]{0:T(1024)(128)(4,1)S(1)}, pred[4096]{0:T(1024)(128)(4,1)}, u32[]{:S(2)}) copy-start(pred[4096]{0:T(1024)(128)(4,1)} %get-tuple-element.221) | copy-start | bytes 12292
  307.5 4.7 %copy-start.18 = (pred[4096]{0:T(1024)(128)(4,1)S(1)}, pred[4096]{0:T(1024)(128)(4,1)}, u32[]{:S(2)}) copy-start(pred[4096]{0:T(1024)(128)(4,1)} %get-tuple-element.219) | copy-start | bytes 12292
  310.5 2.8 copy-start.17
  311.6 2.8 copy-start.16
  312.7 2.8 copy-start.15
  313.8 2.8 copy-start.14
  320.5 4.8 %collective-permute-start.9 = (bf16[3,4,128]{2,1,0:T(4,128)(2,1)S(1)}, bf16[3,4,128]{2,1,0:T(4,128)(2,1)S(1)}, u32[]{:S(2)}, u32[]{:S(2)}) collective-permute-start(bf16[3,4,128]{2,1,0:T(4,128)(2,1)S(1)} %pad_maximum_fusion.9), channel_id=1, source_target_pairs={{28,0},{0,4},{4,8},{8,12},{12,16},{16,20},{20,24},{24,28},{29,1},{... | collective-permute-start | bytes 9224 | tf_op jit(solution)/shard_map/ppermute | solution.py:25
  320.6 4.8 %collective-permute-start.8 = (bf16[3,4,128]{2,1,0:T(4,128)(2,1)S(1)}, bf16[3,4,128]{2,1,0:T(4,128)(2,1)S(1)}, u32[]{:S(2)}, u32[]{:S(2)}) collective-permute-start(bf16[3,4,128]{2,1,0:T(4,128)(2,1)S(1)} %pad_maximum_fusion.8), channel_id=1, source_target_pairs={{4,0},{8,4},{12,8},{16,12},{20,16},{24,20},{28,24},{0,28},{5,1},{9... | collective-permute-start | bytes 9224 | tf_op jit(solution)/shard_map/ppermute | solution.py:25
  325.4 4.8 %collective-permute-start.10 = (bf16[3,4,128]{2,1,0:T(4,128)(2,1)S(1)}, bf16[3,4,128]{2,1,0:T(4,128)(2,1)S(1)}, u32[]{:S(2)}, u32[]{:S(2)}) collective-permute-start(bf16[3,4,128]{2,1,0:T(4,128)(2,1)S(1)} %pad_maximum_fusion.10), channel_id=1, source_target_pairs={{1,0},{2,1},{3,2},{0,3},{5,4},{6,5},{7,6},{4,7},{9,8},{10,9},{11,1... | collective-permute-start | bytes 9224 | tf_op jit(solution)/shard_map/ppermute | solution.py:25
  328.9 6.3 %collective-permute-start.5 = (bf16[3,128,128]{2,1,0:T(8,128)(2,1)S(1)}, bf16[3,128,128]{2,1,0:T(8,128)(2,1)S(1)}, u32[]{:S(2)}, u32[]{:S(2)}) collective-permute-start(bf16[3,128,128]{2,1,0:T(8,128)(2,1)S(1)} %pad_maximum_fusion.4), channel_id=1, source_target_pairs={{28,0},{0,4},{4,8},{8,12},{12,16},{16,20},{20,24},{24,28},{29,1},{... | collective-permute-start | bytes 294920 | tf_op jit(solution)/shard_map/ppermute | solution.py:25
  330.2 4.8 %collective-permute-start.11 = (bf16[3,4,128]{2,1,0:T(4,128)(2,1)S(1)}, bf16[3,4,128]{2,1,0:T(4,128)(2,1)S(1)}, u32[]{:S(2)}, u32[]{:S(2)}) collective-permute-start(bf16[3,4,128]{2,1,0:T(4,128)(2,1)S(1)} %pad_maximum_fusion.11), channel_id=1, source_target_pairs={{3,0},{0,1},{1,2},{2,3},{7,4},{4,5},{5,6},{6,7},{11,8},{8,9},{9,10... | collective-permute-start | bytes 9224 | tf_op jit(solution)/shard_map/ppermute | solution.py:25
  332.3 4.5 %collective-permute-start.4 = (bf16[3,128,128]{2,1,0:T(8,128)(2,1)S(1)}, bf16[3,128,128]{2,1,0:T(8,128)(2,1)S(1)}, u32[]{:S(2)}, u32[]{:S(2)}) collective-permute-start(bf16[3,128,128]{2,1,0:T(8,128)(2,1)S(1)} %pad_maximum_fusion.3), channel_id=1, source_target_pairs={{4,0},{8,4},{12,8},{16,12},{20,16},{24,20},{28,24},{0,28},{5,1},{9... | collective-permute-start | bytes 294920 | tf_op jit(solution)/shard_map/ppermute | solution.py:25
  336.8 4.7 %collective-permute-start.6 = (bf16[3,128,128]{2,1,0:T(8,128)(2,1)S(1)}, bf16[3,128,128]{2,1,0:T(8,128)(2,1)S(1)}, u32[]{:S(2)}, u32[]{:S(2)}) collective-permute-start(bf16[3,128,128]{2,1,0:T(8,128)(2,1)S(1)} %pad_maximum_fusion.5), channel_id=1, source_target_pairs={{1,0},{2,1},{3,2},{0,3},{5,4},{6,5},{7,6},{4,7},{9,8},{10,9},{11,1... | collective-permute-start | bytes 294920 | tf_op jit(solution)/shard_map/ppermute | solution.py:25
  341.5 5.6 %collective-permute-start.7 = (bf16[3,128,128]{2,1,0:T(8,128)(2,1)S(1)}, bf16[3,128,128]{2,1,0:T(8,128)(2,1)S(1)}, u32[]{:S(2)}, u32[]{:S(2)}) collective-permute-start(bf16[3,128,128]{2,1,0:T(8,128)(2,1)S(1)} %pad_maximum_fusion.6), channel_id=1, source_target_pairs={{3,0},{0,1},{1,2},{2,3},{7,4},{4,5},{5,6},{6,7},{11,8},{8,9},{9,10... | collective-permute-start | bytes 294920 | tf_op jit(solution)/shard_map/ppermute | solution.py:25
  347.2 0.7 copy-start.13
where the time goes:
time: 350 us; the launch traced here: 348 us
  matrix products  189 us (54%)
  blocking collectives  40.4 us (12%)
  other arithmetic  34 us (10%)
  local copies, waits for them, and re-layouts  28.1 us (8%)
  starting transfers between devices  22.2 us (6%)
  waiting for transfers between devices  17.2 us (5%)
  loops' own time  16 us (5%)
    dot_general x8, matrix products, particle_one_group(): lax.dot_general(recv_hot.astype(jnp.float32), message, (((0,), (0,)), (()...  55.3 us
    psum x1, blocking collectives, shards(): lax.psum((jnp.sum(mass[None, :] * vel1, axis=1), jnp.sum(mass)), ('gx', '...  40.4 us
    dot_general x8, matrix products, particle_one_group(): message = jnp.dot(act, w_edge, preferred_element_type=jnp.float32)  33.7 us
    dot_general x8, matrix products, encode_one_group(): lax.dot_general(onehot, rows, (((0,), (0,)), ((), ())), preferred_element...  24.5 us
    dot_general x8, matrix products, particle_one_group(): jnp.dot(recv_hot, proj_part[:, width:], preferred_element_type=jnp.float32)  20.6 us
    dot_general x1, matrix products, mesh_update(): jnp.dot(summed, w_mesh, preferred_element_type=jnp.float32)  19.7 us
    dot_general x8, matrix products, particle_one_group(): jnp.dot(near, w_node[width:], preferred_element_type=jnp.float32)  16.9 us
    dynamic_slice x16, local copies, waits for them, and re-layouts, encode(): lax.map(encode_one_group, (feat_g, cell_g, numbers)).reshape(-1, width)  14.6 us
  transfers between devices with their start and end apart: 12, of which 10 were waited for; matrix products, arithmetic and copies ran while one was open for 2% of the time, Pallas kernels for 0%

commit v1 on v0

v1 whole, which is shorter than its diff:
```python
import functools
import jax
import jax.numpy as jnp
from jax import lax
from jax.experimental import pallas as pl
from jax.experimental.pallas import tpu as pltpu
from jax.sharding import PartitionSpec as P

directions = ((-1, -1), (-1, 0), (-1, 1), (0, -1), (0, 1), (1, -1), (1, 0), (1, 1))
LANES = 128
VMEM_LIMIT = 60 * 1024 * 1024


def from_behind(block, axis, distance):
    devices = range(lax.axis_size(axis))
    route = [((i - distance) % len(devices), i) for i in devices]
    return lax.ppermute(block, axis, route)


def summed_over(total, axis):
    devices = lax.axis_size(axis)
    if devices & (devices - 1):
        return lax.psum(total, axis)
    distance = 1
    while distance < devices:
        total = total + from_behind(total, axis, distance)
        distance *= 2
    return total


def group_sizes(parts, cells):
    members = min(512, parts)
    count = parts // members
    return (members, count, cells // count)


def silu(v):
    half = 0.5 * v
    return half + half * jnp.tanh(half)


def f32dot(a, b):
    return jnp.dot(a, b, preferred_element_type=jnp.float32)


def row_hot(keys, rows, first):
    lanes = lax.broadcasted_iota(jnp.int32, (rows, keys.shape[1]), 0) + first
    return jnp.where(lanes == keys, 1.0, 0.0).astype(jnp.bfloat16)


def col_hot(cols, start, stop, width):
    lanes = lax.broadcasted_iota(jnp.int32, (LANES, width), 1)
    parts = [
        jnp.where(lanes == cols[:, j : j + 1], 1.0, 0.0).astype(jnp.bfloat16)
        for j in range(start, stop)
    ]
    return jnp.concatenate(parts, axis=0)


def encode_kernel(chunk, cell_ref, feat_ref, state_ref, w_enc_ref, out_ref):
    span = state_ref.shape[0]
    base = pl.program_id(0) * span
    cells = cell_ref[0] - base

    def body(i, carry):
        first = pl.multiple_of(i * chunk, chunk)
        onehot = row_hot(cells, chunk, first)
        deposit = f32dot(onehot, feat_ref[...]).astype(jnp.bfloat16)
        rows = pl.ds(first, chunk)
        out_ref[rows, :] = (
            state_ref[rows, :].astype(jnp.float32) + f32dot(deposit, w_enc_ref[...])
        ).astype(jnp.bfloat16)
        return carry

    lax.fori_loop(0, span // chunk, body, 0)


def edge_kernel(
    members, send_ref, recv_ref, recv_row_ref, feat_ref, w_pair_ref, w_edge_ref, out_ref
):
    base = pl.program_id(0) * members
    width = feat_ref.shape[1]
    proj = f32dot(feat_ref[...], w_pair_ref[...]).astype(jnp.bfloat16)
    table = jnp.concatenate([proj[:, :width], proj[:, width:]], axis=0)
    send_cols = (send_ref[0] - base).T
    recv_cols = (recv_ref[0] - base).T
    turns = send_cols.shape[1]
    step = 6 if turns % 6 == 0 else 1
    total = jnp.zeros((members, width), jnp.float32)
    for start in range(0, turns, step):
        hot = jnp.concatenate(
            [
                col_hot(send_cols, start, start + step, members),
                col_hot(recv_cols, start, start + step, members),
            ],
            axis=1,
        )
        act = silu(f32dot(hot, table)).astype(jnp.bfloat16)
        keys = recv_row_ref[0, :, start * LANES : (start + step) * LANES] - base
        total = total + f32dot(row_hot(keys, members, 0), act)
    edge_sum = f32dot(total.astype(jnp.bfloat16), w_edge_ref[...])
    out_ref[...] = edge_sum.astype(jnp.bfloat16)


def node_kernel(
    plane,
    depth,
    cap,
    below_ref,
    centre_ref,
    above_ref,
    xlo_ref,
    xhi_ref,
    ylo_ref,
    yhi_ref,
    cell_ref,
    dest_ref,
    dest_row_ref,
    edge_ref,
    feat_ref,
    mass_ref,
    vel_ref,
    w_mesh_ref,
    w_node_ref,
    w_accel_ref,
    mesh_ref,
    stay_ref,
    vel1_ref,
    packed_ref,
    total_ref,
    slots_ref,
    carry_ref,
):
    step = pl.program_id(0)
    last = pl.num_programs(0) - 1
    span, width = centre_ref.shape
    members = feat_ref.shape[0]
    planes = span // plane
    base = step * span

    @pl.when(step == 0)
    def _():
        slots_ref[...] = jnp.zeros_like(slots_ref)
        carry_ref[...] = jnp.zeros_like(carry_ref)
        total_ref[...] = jnp.zeros_like(total_ref)

    level = lax.broadcasted_iota(jnp.int32, (plane, width), 0) % depth
    for p in range(planes):
        rows = slice(p * plane, (p + 1) * plane)
        centre = centre_ref[rows, :].astype(jnp.float32)
        if p == 0:
            below = jnp.where(
                step == 0, xlo_ref[...].astype(jnp.float32), below_ref[...].astype(jnp.float32)
            )
        else:
            below = centre_ref[(p - 1) * plane : p * plane, :].astype(jnp.float32)
        if p == planes - 1:
            above = jnp.where(
                step == last, xhi_ref[...].astype(jnp.float32), above_ref[...].astype(jnp.float32)
            )
        else:
            above = centre_ref[(p + 1) * plane : (p + 2) * plane, :].astype(jnp.float32)
        edge = slice(p * depth, (p + 1) * depth)
        left = jnp.concatenate([ylo_ref[edge, :].astype(jnp.float32), centre[:-depth]], axis=0)
        right = jnp.concatenate([centre[depth:], yhi_ref[edge, :].astype(jnp.float32)], axis=0)
        down = jnp.where(level == 0, 0.0, pltpu.roll(centre, 1, 0))
        up = jnp.where(level == depth - 1, 0.0, pltpu.roll(centre, plane - 1, 0))
        sides = (below + above + left + right + (up + down)).astype(jnp.bfloat16)
        mesh_ref[rows, :] = (centre + silu(f32dot(sides, w_mesh_ref[...]))).astype(jnp.bfloat16)

    cell_cols = (cell_ref[0] - base).T
    dest_cols = dest_ref[0].T
    turns = members // LANES
    near = f32dot(col_hot(cell_cols, 0, turns, span), mesh_ref[...]).astype(jnp.bfloat16)
    update = f32dot(edge_ref[...], w_node_ref[:width, :]) + f32dot(near, w_node_ref[width:, :])
    h_new = (feat_ref[...].astype(jnp.float32) + silu(update)).astype(jnp.bfloat16)
    h_wide = h_new.astype(jnp.float32)
    for j in range(turns):
        rows = slice(j * LANES, (j + 1) * LANES)
        stay_ref[rows, :] = jnp.where(dest_cols[:, j : j + 1] == 0, h_wide[rows], 0.0).astype(
            jnp.bfloat16
        )
    accel = lax.dot_general(
        w_accel_ref[...], h_new, (((1,), (1,)), ((), ())), preferred_element_type=jnp.float32
    )
    vel1 = vel_ref[...] + accel[:3]
    mass = mass_ref[0]
    vel1_ref[...] = vel1
    sums = jnp.concatenate([mass * vel1, mass], axis=0)
    total_ref[...] += sum(sums[:, j * LANES : (j + 1) * LANES] for j in range(turns))

    dest = dest_row_ref[0]
    ways = lax.broadcasted_iota(jnp.int32, (8, members), 0) + 1
    chosen_way = jnp.where(ways == dest, 1.0, 0.0)
    earlier = jnp.where(
        lax.broadcasted_iota(jnp.int32, (members, members), 0)
        < lax.broadcasted_iota(jnp.int32, (members, members), 1),
        1.0,
        0.0,
    ).astype(jnp.bfloat16)
    place = f32dot(chosen_way.astype(jnp.bfloat16), earlier) + carry_ref[:, :1]
    slot = jnp.sum(place * chosen_way, axis=0, keepdims=True).astype(jnp.int32)
    carry_ref[...] += jnp.sum(chosen_way, axis=1, keepdims=True)
    key = jnp.where(dest > 0, (dest - 1) * cap + slot, -1)
    extra = jnp.concatenate([vel1, mass, jnp.zeros((LANES - 4, members), jnp.float32)], axis=0)
    values = jnp.concatenate([h_new, extra.T.astype(jnp.bfloat16)], axis=1)
    half = slots_ref.shape[0] // 2
    for first in (0, half):
        rows = slice(first, first + half)
        slots_ref[rows, :] += f32dot(row_hot(key, half, first), values)

    @pl.when(step == last)
    def _():
        moving = slots_ref[:, width:].T
        for k in range(8):
            rows = slice(k * cap, (k + 1) * cap)
            packed_ref[k, :cap, :] = slots_ref[rows, :width].astype(jnp.bfloat16)
            packed_ref[k, cap:, :] = moving[:16, rows].astype(jnp.bfloat16)


def unpack(moving, drift):
    values = moving.astype(jnp.float32)
    weight = values[..., 3:4, :]
    speed = jnp.where(weight > 0, values[..., :3, :] - drift[:, None], 0.0)
    return jnp.concatenate([speed, weight], axis=-2)


def whole(shape):
    return pl.BlockSpec(shape, lambda g: (0,) * len(shape))


def shards(
    mesh_state,
    part_feat,
    cell_index,
    pairs,
    dest,
    mass,
    velocity,
    w_enc,
    w_mesh,
    w_pair,
    w_edge,
    w_node,
    w_accel,
):
    shape = mesh_state.shape
    parts, width = part_feat.shape
    cx, cy, cz, channels = shape
    cells = cx * cy * cz
    plane = cy * cz
    members, count, span = group_sizes(parts, cells)
    planes = span // plane
    per_group = pairs.shape[1] // count
    cap = parts // 32
    bf16, f32 = (jnp.bfloat16, jnp.float32)
    params = pltpu.CompilerParams(vmem_limit_bytes=VMEM_LIMIT)

    by_rows = pl.BlockSpec((members, width), lambda g: (g, 0))
    by_cells = pl.BlockSpec((span, channels), lambda g: (g, 0))
    by_row = pl.BlockSpec((1, 1, members), lambda g: (g, 0, 0))
    by_tile = pl.BlockSpec((1, members // LANES, LANES), lambda g: (g, 0, 0))

    cell_row = cell_index.reshape(count, 1, members)
    cell_tile = cell_index.reshape(count, members // LANES, LANES)
    dest_row = dest.reshape(count, 1, members)
    dest_tile = dest.reshape(count, members // LANES, LANES)
    mass_row = mass.reshape(count, 1, members)
    send_tile = pairs[0].reshape(count, per_group // LANES, LANES)
    recv_tile = pairs[1].reshape(count, per_group // LANES, LANES)
    recv_row = pairs[1].reshape(count, 1, per_group)
    accel8 = jnp.pad(w_accel, ((0, 8 - w_accel.shape[0]), (0, 0)))

    mesh1 = pl.pallas_call(
        functools.partial(encode_kernel, min(512, span)),
        grid=(count,),
        out_shape=jax.ShapeDtypeStruct((cells, channels), bf16),
        in_specs=[by_row, by_rows, by_cells, whole(w_enc.shape)],
        out_specs=by_cells,
        compiler_params=params,
        cost_estimate=pl.CostEstimate(
            flops=2 * cells * members * width, bytes_accessed=4 * cells * channels, transcendentals=0
        ),
        name="encode",
    )(cell_row, part_feat, mesh_state.reshape(cells, channels), w_enc)

    grid1 = mesh1.reshape(shape)
    xlo = from_behind(grid1[cx - 1 :].reshape(plane, channels), "gx", 1)
    xhi = from_behind(grid1[:1].reshape(plane, channels), "gx", -1)
    ylo = from_behind(grid1[:, cy - 1 :].reshape(cx * cz, channels), "gy", 1)
    yhi = from_behind(grid1[:, :1].reshape(cx * cz, channels), "gy", -1)

    by_pairs = pl.BlockSpec((1, per_group // LANES, LANES), lambda g: (g, 0, 0))
    edge_sum = pl.pallas_call(
        functools.partial(edge_kernel, members),
        grid=(count,),
        out_shape=jax.ShapeDtypeStruct((parts, width), bf16),
        in_specs=[
            by_pairs,
            by_pairs,
            pl.BlockSpec((1, 1, per_group), lambda g: (g, 0, 0)),
            by_rows,
            whole(w_pair.shape),
            whole(w_edge.shape),
        ],
        out_specs=by_rows,
        compiler_params=params,
        cost_estimate=pl.CostEstimate(
            flops=6 * pairs.shape[1] * members * width,
            bytes_accessed=4 * parts * width,
            transcendentals=pairs.shape[1] * width,
        ),
        name="edges",
    )(send_tile, recv_tile, recv_row, part_feat, w_pair, w_edge)

    one_plane = lambda f: pl.BlockSpec((plane, channels), f)
    by_layer = pl.BlockSpec((planes * cz, channels), lambda g: (g, 0))
    by_speed = pl.BlockSpec((3, members), lambda g: (0, g))
    mesh2, stay_feat, vel1, packed, totals = pl.pallas_call(
        functools.partial(node_kernel, plane, cz, cap),
        grid=(count,),
        out_shape=(
            jax.ShapeDtypeStruct((cells, channels), bf16),
            jax.ShapeDtypeStruct((parts, width), bf16),
            jax.ShapeDtypeStruct((3, parts), f32),
            jax.ShapeDtypeStruct((8, cap + 16, width), bf16),
            jax.ShapeDtypeStruct((4, LANES), f32),
        ),
        in_specs=[
            one_plane(lambda g: (jnp.maximum(g * planes - 1, 0), 0)),
            by_cells,
            one_plane(lambda g: (jnp.minimum(g * planes + planes, cx - 1), 0)),
            whole((plane, channels)),
            whole((plane, channels)),
            by_layer,
            by_layer,
            by_tile,
            by_tile,
            by_row,
            by_rows,
            by_rows,
            by_row,
            by_speed,
            whole(w_mesh.shape),
            whole(w_node.shape),
            whole(accel8.shape),
        ],
        out_specs=(
            by_cells,
            by_rows,
            by_speed,
            whole((8, cap + 16, width)),
            whole((4, LANES)),
        ),
        scratch_shapes=[
            pltpu.VMEM((8 * cap, width + LANES), f32),
            pltpu.VMEM((8, LANES), f32),
        ],
        compiler_params=params,
        name="nodes",
    )(
        mesh1,
        mesh1,
        mesh1,
        xlo,
        xhi,
        ylo,
        yhi,
        cell_tile,
        dest_tile,
        dest_row,
        edge_sum,
        part_feat,
        mass_row,
        velocity,
        w_mesh,
        w_node,
        accel8,
    )

    sums = jnp.sum(summed_over(summed_over(totals, "gx"), "gy"), axis=1)
    drift = sums[:3] / sums[3]
    stay_vel = jnp.where((dest == 0)[None, :], vel1 - drift[:, None], 0.0)

    got = [packed[k] for k in range(8)]
    for axis, part in (("gx", 0), ("gy", 1)):
        for distance in (1, -1):
            chosen = [k for k, offset in enumerate(directions) if offset[part] == distance]
            moved = from_behind(jnp.stack([got[k] for k in chosen], axis=0), axis, distance)
            for place, k in enumerate(chosen):
                got[k] = moved[place]
    arrived = jnp.stack(got, axis=0)
    arrived_feat = arrived[:, :cap].reshape(-1, width)
    arrived_vel = unpack(arrived[:, cap : cap + 4], drift).transpose(1, 0, 2).reshape(4, -1)
    return (mesh2.reshape(shape), stay_feat, stay_vel, arrived_feat, arrived_vel)


def solution(mesh):
    placed = (
        P("gx", "gy", None, None),
        P(("gx", "gy"), None),
        P(("gx", "gy")),
        P(None, ("gx", "gy")),
        P(("gx", "gy")),
        P(("gx", "gy")),
        P(None, ("gx", "gy")),
        P(),
        P(),
        P(),
        P(),
        P(),
        P(),
    )
    return jax.shard_map(
        shards,
        mesh=mesh,
        in_specs=placed,
        out_specs=(
            P("gx", "gy", None, None),
            P(("gx", "gy"), None),
            P(None, ("gx", "gy")),
            P(("gx", "gy"), None),
            P(None, ("gx", "gy")),
        ),
        check_vma=False,
    )
```

time: 350 us -> 128 us (0.37)
  matrix products: 189 us -> 0 us
  Pallas kernels: 0 us -> 73.8 us
  blocking collectives: 40.4 us -> 0 us
  other arithmetic: 34 us -> 3.75 us
  local copies, waits for them, and re-layouts: 28.1 us -> 7.47 us
  loops' own time: 16 us -> 0 us
  waiting for transfers between devices: 17.2 us -> 25.7 us
  starting transfers between devices: 22.2 us -> 15.9 us
    dot_general x68 -> x0, matrix products: 189 us -> none  [the longest x8 55.3 us: particle_one_group(): lax.dot_general(recv_hot.astype(jnp.float32), message, (((0,), (0,)), (()...]
    pallas_call x0 -> x3, Pallas kernels: none -> 73.8 us  [the longest x1 29.5 us: shards(): pl.pallas_call(functools.partial(edge_kernel, members), grid=(count,), ou...]
    psum x1 -> x0, blocking collectives: 40.4 us -> none  [shards(): lax.psum((jnp.sum(mass[None, :] * vel1, axis=1), jnp.sum(mass)), ('gx', '...]
    sub x24 -> x0, other arithmetic: 17.5 us -> none  [the longest x8 11.5 us: particle_one_group(): pair_part[0] - base]
    another operation x2 -> x0, loops' own time: 16 us -> none  [the longest x1 10.7 us: particle_step(): lax.scan(particle_one_group, 0, (proj_g, feat_g, pair_g, cell_g, rows_g,...]
    dynamic_slice x16 -> x0, local copies, waits for them, and re-layouts: 14.6 us -> none  [encode(): lax.map(encode_one_group, (feat_g, cell_g, numbers)).reshape(-1, width)]
    ppermute x8 -> x13, waiting for transfers between devices: 11.1 us -> 25.7 us  [from_behind(): return lax.ppermute(block, axis, route)]
    ppermute x4 -> x0, starting transfers between devices: 7.76 us -> none  [the longest x2 5.07 us: padded_2(): after = lax.ppermute(initial, axis, down)]
  transfers between devices with their start and end apart: 12 -> 13, of which waited for: 10 -> 7; matrix products, arithmetic and copies ran while one was open for 2% -> 6% of each run, Pallas kernels for 0% -> 23%
where the time goes in v1:
time: 128 us; the launch traced here: 127 us
  Pallas kernels  73.8 us (58%)
  waiting for transfers between devices  25.7 us (20%)
  starting transfers between devices  15.9 us (12%)
  local copies, waits for them, and re-layouts  7.47 us (6%)
  other arithmetic  3.75 us (3%)
    pallas_call x1, Pallas kernels, shards(): pl.pallas_call(functools.partial(edge_kernel, members), grid=(count,), ou...  29.5 us
    pallas_call x1, Pallas kernels, shards(): pl.pallas_call(functools.partial(node_kernel, plane, cz, cap), grid=(coun...  27.4 us
    ppermute x13, waiting for transfers between devices, from_behind(): return lax.ppermute(block, axis, route)  25.7 us
    pallas_call x1, Pallas kernels, shards(): pl.pallas_call(functools.partial(encode_kernel, min(512, span)), grid=(co...  17 us
    ppermute x13, starting transfers between devices, from_behind(): return lax.ppermute(block, axis, route)  15.9 us
  transfers between devices with their start and end apart: 13, of which 7 were waited for; matrix products, arithmetic and copies ran while one was open for 6% of the time, Pallas kernels for 23%

profile of v1, /device:TPU:0, one launch (start us, length us, event | category | flops | bytes accessed | tf_op | source)
XLA Modules:
  0.0 127.4 jit_solution(14718468751108511670)
XLA Ops:
  0.6 0.0 copy-start.2
  0.6 17.0 %encode.1.below_ref.centre_ref.above_ref = bf16[16384,128]{1,0:T(8,128)(2,1)} custom-call(s32[8,1,512]{2,1,0:T(1,128)} %bitcast.36, bf16[4096,128]{1,0:T(8,128)(2,1)} %feat_ref.5, bf16[16384,128]{1,0:T(8,128)(2,1)} %bitcast.27, bf16[128,128]{1,0:T(8,128)(2,1)} %w_enc_ref.1), custom_call_target="tpu_custom_call" | custom-call | flops 2147483648 | bytes 8388608 | tf_op jit(solution)/shard_map/encode/pallas_call | solution.py:274
  17.6 1.1 fusion.2
  18.7 0.5 collective-permute-start
  19.2 4.1 %collective-permute-start.1 = (bf16[1024,128]{1,0:T(8,128)(2,1)S(1)}, bf16[1024,128]{1,0:T(8,128)(2,1)S(1)}, u32[]{:S(2)}, u32[]{:S(2)}) collective-permute-start(bf16[1024,128]{1,0:T(8,128)(2,1)S(1)} %get-tuple-element.17), channel_id=1, source_target_pairs={{4,0},{8,4},{12,8},{16,12},{20,16},{24,20},{28,24},{0,28},{5,1},{9... | collective-permute-start | bytes 786440 | tf_op jit(solution)/shard_map/ppermute | solution.py:17
  23.3 1.0 fusion.1
  24.3 2.0 %collective-permute-start.2 = (bf16[512,128]{1,0:T(8,128)(2,1)S(1)}, bf16[512,128]{1,0:T(8,128)(2,1)S(1)}, u32[]{:S(2)}, u32[]{:S(2)}) collective-permute-start(bf16[512,128]{1,0:T(8,128)(2,1)S(1)} %bitcast.32), channel_id=1, source_target_pairs={{3,0},{0,1},{1,2},{2,3},{7,4},{4,5},{5,6},{6,7},{11,8},{8,9},{9,10... | collective-permute-start | bytes 393224 | tf_op jit(solution)/shard_map/ppermute | solution.py:17
  26.3 1.0 collective-permute-start.3
  27.3 0.0 copy-done.2
  27.3 0.8 fusion.5
  28.1 0.0 copy-start.6
  28.1 29.5 %edges.1.edge_ref = bf16[4096,128]{1,0:T(8,128)(2,1)} custom-call(s32[8,24,128]{2,1,0:T(8,128)} %bitcast.35, s32[8,24,128]{2,1,0:T(8,128)} %bitcast.33, s32[8,1,3072]{2,1,0:T(1,128)} %bitcast.34, bf16[4096,128]{1,0:T(8,128)(2,1)} %feat_ref.5, bf16[128,256]{1,0:T(8,128)(2,1)} %w_pair_ref.1, bf16[128,128]{1,0:T(8,128)(2,1)} %w_edge_ref.1), custom_call_target="tpu_custom_call" | custom-call | flops 9663676416 | bytes 2097152 | tf_op jit(solution)/shard_map/edges/pallas_call | solution.py:294
  57.6 0.0 copy-done.6
  57.6 0.6 pad.4.w_accel_ref
  58.2 0.0 collective-permute-done.2.ylo_ref
  58.2 0.0 copy-start.4
  58.2 0.0 collective-permute-done.3.yhi_ref
  58.2 0.0 copy-start.5
  58.2 0.0 collective-permute-done.xlo_ref
  58.2 0.0 copy-start
  58.2 0.0 collective-permute-done.1.xhi_ref
  58.2 0.0 copy-start.1
  58.2 0.6 copy-done.4
  58.8 0.0 copy-done.5
  58.9 0.1 copy-done
  59.0 0.1 copy-done.1
  59.1 0.0 copy-start.3
  59.1 27.4 %nodes.1 = (bf16[16384,128]{1,0:T(8,128)(2,1)}, bf16[4096,128]{1,0:T(8,128)(2,1)}, f32[3,4096]{1,0:T(4,128)}, bf16[8,144,128]{2,1,0:T(8,128)(2,1)}, f32[4,128]{1,0:T(4,128)}) custom-call(bf16[16384,128]{1,0:T(8,128)(2,1)} %encode.1.below_ref.centre_ref.above_ref, bf16[16384,128]{1,0:T(8,128)(2,1)} %encode.1.below_ref.centre_ref.above_ref, ...), custom_call_target="tpu_custom_call" | custom-call | tf_op jit(solution)/shard_map/nodes/pallas_call | solution.py:319
  86.5 0.1 collective-permute-start.4
  86.5 5.0 %collective-permute-done.4 = f32[4,128]{1,0:T(4,128)S(1)} collective-permute-done((f32[4,128]{1,0:T(4,128)}, f32[4,128]{1,0:T(4,128)S(1)}, u32[]{:S(2)}, u32[]{:S(2)}) %collective-permute-start.4) | collective-permute-done | bytes 2080 | tf_op jit(solution)/shard_map/ppermute | solution.py:17
  91.5 0.7 add.17
  92.2 0.0 collective-permute-start.5
  92.2 5.4 %collective-permute-done.5 = f32[4,128]{1,0:T(4,128)S(1)} collective-permute-done((f32[4,128]{1,0:T(4,128)S(1)}, f32[4,128]{1,0:T(4,128)S(1)}, u32[]{:S(2)}, u32[]{:S(2)}) %collective-permute-start.5) | collective-permute-done | bytes 2080 | tf_op jit(solution)/shard_map/ppermute | solution.py:17
  97.6 0.0 collective-permute-start.6
  97.6 0.0 copy-done.3
  97.6 4.5 %collective-permute-done.6 = f32[4,128]{1,0:T(4,128)S(1)} collective-permute-done((f32[4,128]{1,0:T(4,128)S(1)}, f32[4,128]{1,0:T(4,128)S(1)}, u32[]{:S(2)}, u32[]{:S(2)}) %collective-permute-start.6) | collective-permute-done | bytes 2080 | tf_op jit(solution)/shard_map/ppermute | solution.py:17
  102.1 1.0 collective-permute-start.7
  103.1 1.0 fusion.4
  104.1 2.5 %collective-permute-done.7 = f32[4,128]{1,0:T(4,128)S(1)} collective-permute-done((f32[4,128]{1,0:T(4,128)S(1)}, f32[4,128]{1,0:T(4,128)S(1)}, u32[]{:S(2)}, u32[]{:S(2)}) %collective-permute-start.7) | collective-permute-done | bytes 2080 | tf_op jit(solution)/shard_map/ppermute | solution.py:17
  106.6 1.9 %collective-permute-start.8 = (f32[4,128]{1,0:T(4,128)S(1)}, f32[4,128]{1,0:T(4,128)S(1)}, u32[]{:S(2)}, u32[]{:S(2)}) collective-permute-start(f32[4,128]{1,0:T(4,128)S(1)} %add.20), channel_id=1, source_target_pairs={{2,0},{3,1},{0,2},{1,3},{6,4},{7,5},{4,6},{5,7},{10,8},{11,9},{8,1... | collective-permute-start | bytes 6152 | tf_op jit(solution)/shard_map/ppermute | solution.py:17
  108.5 0.8 fusion.3
  109.3 0.0 collective-permute-start.10
  109.3 3.5 %collective-permute-start.9 = (bf16[3,144,128]{2,1,0:T(8,128)(2,1)S(1)}, bf16[3,144,128]{2,1,0:T(8,128)(2,1)S(1)}, u32[]{:S(2)}, u32[]{:S(2)}) collective-permute-start(bf16[3,144,128]{2,1,0:T(8,128)(2,1)S(1)} %get-tuple-element.21), channel_id=1, source_target_pairs={{4,0},{8,4},{12,8},{16,12},{20,16},{24,20},{28,24},{0,28},{5,1},{9... | collective-permute-start | bytes 331784 | tf_op jit(solution)/shard_map/ppermute | solution.py:17
  112.9 0.0 collective-permute-done.8
  112.9 0.1 add_reduce_fusion
  113.0 0.6 slice.100
  113.6 1.7 %collective-permute-done.10 = bf16[3,144,128]{2,1,0:T(8,128)(2,1)S(1)} collective-permute-done((bf16[3,144,128]{2,1,0:T(8,128)(2,1)S(1)}, bf16[3,144,128]{2,1,0:T(8,128)(2,1)S(1)}, u32[]{:S(2)}, u32[]{:S(2)}) %collective-permute-start.10) | collective-permute-done | bytes 110624 | tf_op jit(solution)/shard_map/ppermute | solution.py:17
  115.3 0.0 collective-permute-done.9
  115.3 0.1 collective-permute-start.11
  115.4 0.7 slice_divide_fusion
  116.1 4.1 %collective-permute-done.11 = bf16[3,144,128]{2,1,0:T(8,128)(2,1)S(1)} collective-permute-done((bf16[3,144,128]{2,1,0:T(8,128)(2,1)S(1)}, bf16[3,144,128]{2,1,0:T(8,128)(2,1)S(1)}, u32[]{:S(2)}, u32[]{:S(2)}) %collective-permute-start.11) | collective-permute-done | bytes 110624 | tf_op jit(solution)/shard_map/ppermute | solution.py:17
  120.2 1.6 %collective-permute-start.12 = (bf16[3,144,128]{2,1,0:T(8,128)(2,1)S(1)}, bf16[3,144,128]{2,1,0:T(8,128)(2,1)S(1)}, u32[]{:S(2)}, u32[]{:S(2)}) collective-permute-start(bf16[3,144,128]{2,1,0:T(8,128)(2,1)S(1)} %pad_maximum_fusion.1), channel_id=1, source_target_pairs={{3,0},{0,1},{1,2},{2,3},{7,4},{4,5},{5,6},{6,7},{11,8},{8,9},{9,10... | collective-permute-start | bytes 331784 | tf_op jit(solution)/shard_map/ppermute | solution.py:17
  121.8 1.5 %subtract_select_fusion = f32[3,4096]{1,0:T(4,128)} fusion(f32[3,4096]{1,0:T(4,128)} %get-tuple-element.12, f32[3]{0:T(128)S(1)} %slice_divide_fusion, pred[4096]{0:T(1024)(128)(4,1)S(1)} %broadcast_compare_fusion), kind=kLoop, calls=%fused_computation.2 | loop fusion | flops 24576 | bytes 102412 | tf_op jit(solution)/shard_map/jit(_where)/select_n | solution.py:383
  123.4 2.5 %collective-permute-done.12 = bf16[3,144,128]{2,1,0:T(8,128)(2,1)S(1)} collective-permute-done((bf16[3,144,128]{2,1,0:T(8,128)(2,1)S(1)}, bf16[3,144,128]{2,1,0:T(8,128)(2,1)S(1)}, u32[]{:S(2)}, u32[]{:S(2)}) %collective-permute-start.12) | collective-permute-done | bytes 110624 | tf_op jit(solution)/shard_map/ppermute | solution.py:17
  126.0 0.7 slice.137
  126.7 0.1 fusion
  126.8 0.6 maximum_bitcast_fusion
  (20 shorter events, 0.2 us)
Async XLA Ops:
  0.6 26.7 %copy-start.2 = (s32[2,24576]{1,0:T(2,128)S(1)}, s32[2,24576]{1,0:T(2,128)}, u32[]{:S(2)}) copy-start(s32[2,24576]{1,0:T(2,128)} %param.16) | copy-start | bytes 589828
  18.7 39.5 %collective-permute-start = (bf16[1024,128]{1,0:T(8,128)(2,1)S(1)}, bf16[1024,128]{1,0:T(8,128)(2,1)S(1)}, u32[]{:S(2)}, u32[]{:S(2)}) collective-permute-start(bf16[1024,128]{1,0:T(8,128)(2,1)S(1)} %get-tuple-element.18), channel_id=1, source_target_pairs={{28,0},{0,4},{4,8},{8,12},{12,16},{16,20},{20,24},{24,28},{29,1},{... | collective-permute-start | bytes 786440 | tf_op jit(solution)/shard_map/ppermute | solution.py:17
  19.2 39.0 %collective-permute-start.1 = (bf16[1024,128]{1,0:T(8,128)(2,1)S(1)}, bf16[1024,128]{1,0:T(8,128)(2,1)S(1)}, u32[]{:S(2)}, u32[]{:S(2)}) collective-permute-start(bf16[1024,128]{1,0:T(8,128)(2,1)S(1)} %get-tuple-element.17), channel_id=1, source_target_pairs={{4,0},{8,4},{12,8},{16,12},{20,16},{24,20},{28,24},{0,28},{5,1},{9... | collective-permute-start | bytes 786440 | tf_op jit(solution)/shard_map/ppermute | solution.py:17
  24.3 33.9 %collective-permute-start.2 = (bf16[512,128]{1,0:T(8,128)(2,1)S(1)}, bf16[512,128]{1,0:T(8,128)(2,1)S(1)}, u32[]{:S(2)}, u32[]{:S(2)}) collective-permute-start(bf16[512,128]{1,0:T(8,128)(2,1)S(1)} %bitcast.32), channel_id=1, source_target_pairs={{3,0},{0,1},{1,2},{2,3},{7,4},{4,5},{5,6},{6,7},{11,8},{8,9},{9,10... | collective-permute-start | bytes 393224 | tf_op jit(solution)/shard_map/ppermute | solution.py:17
  26.3 31.9 %collective-permute-start.3 = (bf16[512,128]{1,0:T(8,128)(2,1)S(1)}, bf16[512,128]{1,0:T(8,128)(2,1)S(1)}, u32[]{:S(2)}, u32[]{:S(2)}) collective-permute-start(bf16[512,128]{1,0:T(8,128)(2,1)S(1)} %bitcast.31), channel_id=1, source_target_pairs={{1,0},{2,1},{3,2},{0,3},{5,4},{6,5},{7,6},{4,7},{9,8},{10,9},{11,1... | collective-permute-start | bytes 393224 | tf_op jit(solution)/shard_map/ppermute | solution.py:17
  28.1 29.5 %copy-start.6 = (bf16[3,128]{1,0:T(4,128)(2,1)S(1)}, bf16[3,128]{1,0:T(4,128)(2,1)}, u32[]{:S(2)}) copy-start(bf16[3,128]{1,0:T(4,128)(2,1)} %param.25) | copy-start | bytes 2308
  58.2 0.7 copy-start.4
  58.2 0.7 copy-start.5
  58.2 0.8 copy-start
  58.2 0.8 copy-start.1
  59.1 38.5 %copy-start.3 = (s32[4096]{0:T(1024)S(1)}, s32[4096]{0:T(1024)}, u32[]{:S(2)}) copy-start(s32[4096]{0:T(1024)} %param.17) | copy-start | bytes 49156
  86.5 5.1 %collective-permute-start.4 = (f32[4,128]{1,0:T(4,128)}, f32[4,128]{1,0:T(4,128)S(1)}, u32[]{:S(2)}, u32[]{:S(2)}) collective-permute-start(f32[4,128]{1,0:T(4,128)} %get-tuple-element.13), channel_id=1, source_target_pairs={{28,0},{0,4},{4,8},{8,12},{12,16},{16,20},{20,24},{24,28},{29,1},{... | collective-permute-start | bytes 6152 | tf_op jit(solution)/shard_map/ppermute | solution.py:17
  92.2 5.4 %collective-permute-start.5 = (f32[4,128]{1,0:T(4,128)S(1)}, f32[4,128]{1,0:T(4,128)S(1)}, u32[]{:S(2)}, u32[]{:S(2)}) collective-permute-start(f32[4,128]{1,0:T(4,128)S(1)} %add.17), channel_id=1, source_target_pairs={{24,0},{28,4},{0,8},{4,12},{8,16},{12,20},{16,24},{20,28},{25,1},{... | collective-permute-start | bytes 6152 | tf_op jit(solution)/shard_map/ppermute | solution.py:17
  97.6 4.5 %collective-permute-start.6 = (f32[4,128]{1,0:T(4,128)S(1)}, f32[4,128]{1,0:T(4,128)S(1)}, u32[]{:S(2)}, u32[]{:S(2)}) collective-permute-start(f32[4,128]{1,0:T(4,128)S(1)} %add.18), channel_id=1, source_target_pairs={{16,0},{20,4},{24,8},{28,12},{0,16},{4,20},{8,24},{12,28},{17,1},{... | collective-permute-start | bytes 6152 | tf_op jit(solution)/shard_map/ppermute | solution.py:17
  102.1 4.5 %collective-permute-start.7 = (f32[4,128]{1,0:T(4,128)S(1)}, f32[4,128]{1,0:T(4,128)S(1)}, u32[]{:S(2)}, u32[]{:S(2)}) collective-permute-start(f32[4,128]{1,0:T(4,128)S(1)} %add.19), channel_id=1, source_target_pairs={{3,0},{0,1},{1,2},{2,3},{7,4},{4,5},{5,6},{6,7},{11,8},{8,9},{9,10... | collective-permute-start | bytes 6152 | tf_op jit(solution)/shard_map/ppermute | solution.py:17
  106.6 6.3 %collective-permute-start.8 = (f32[4,128]{1,0:T(4,128)S(1)}, f32[4,128]{1,0:T(4,128)S(1)}, u32[]{:S(2)}, u32[]{:S(2)}) collective-permute-start(f32[4,128]{1,0:T(4,128)S(1)} %add.20), channel_id=1, source_target_pairs={{2,0},{3,1},{0,2},{1,3},{6,4},{7,5},{4,6},{5,7},{10,8},{11,9},{8,1... | collective-permute-start | bytes 6152 | tf_op jit(solution)/shard_map/ppermute | solution.py:17
  109.3 6.0 %collective-permute-start.10 = (bf16[3,144,128]{2,1,0:T(8,128)(2,1)S(1)}, bf16[3,144,128]{2,1,0:T(8,128)(2,1)S(1)}, u32[]{:S(2)}, u32[]{:S(2)}) collective-permute-start(bf16[3,144,128]{2,1,0:T(8,128)(2,1)S(1)} %get-tuple-element.22), channel_id=1, source_target_pairs={{28,0},{0,4},{4,8},{8,12},{12,16},{16,20},{20,24},{24,28},{29,1},{... | collective-permute-start | bytes 331784 | tf_op jit(solution)/shard_map/ppermute | solution.py:17
  109.3 6.0 %collective-permute-start.9 = (bf16[3,144,128]{2,1,0:T(8,128)(2,1)S(1)}, bf16[3,144,128]{2,1,0:T(8,128)(2,1)S(1)}, u32[]{:S(2)}, u32[]{:S(2)}) collective-permute-start(bf16[3,144,128]{2,1,0:T(8,128)(2,1)S(1)} %get-tuple-element.21), channel_id=1, source_target_pairs={{4,0},{8,4},{12,8},{16,12},{20,16},{24,20},{28,24},{0,28},{5,1},{9... | collective-permute-start | bytes 331784 | tf_op jit(solution)/shard_map/ppermute | solution.py:17
  115.3 4.8 %collective-permute-start.11 = (bf16[3,144,128]{2,1,0:T(8,128)(2,1)S(1)}, bf16[3,144,128]{2,1,0:T(8,128)(2,1)S(1)}, u32[]{:S(2)}, u32[]{:S(2)}) collective-permute-start(bf16[3,144,128]{2,1,0:T(8,128)(2,1)S(1)} %pad_maximum_fusion), channel_id=1, source_target_pairs={{1,0},{2,1},{3,2},{0,3},{5,4},{6,5},{7,6},{4,7},{9,8},{10,9},{11,1... | collective-permute-start | bytes 331784 | tf_op jit(solution)/shard_map/ppermute | solution.py:17
  120.2 5.7 %collective-permute-start.12 = (bf16[3,144,128]{2,1,0:T(8,128)(2,1)S(1)}, bf16[3,144,128]{2,1,0:T(8,128)(2,1)S(1)}, u32[]{:S(2)}, u32[]{:S(2)}) collective-permute-start(bf16[3,144,128]{2,1,0:T(8,128)(2,1)S(1)} %pad_maximum_fusion.1), channel_id=1, source_target_pairs={{3,0},{0,1},{1,2},{2,3},{7,4},{4,5},{5,6},{6,7},{11,8},{8,9},{9,10... | collective-permute-start | bytes 331784 | tf_op jit(solution)/shard_map/ppermute | solution.py:17
